TPU v7x, 32 devices: a whole 2x2x4 slice. The times are simulated.
32 devices in a mesh: dev: 16 (over z, y, core), rhs: 2 (over x).
Axes of the slice: x: 2, y: 2, z: 4, core: 2. Of those that a mesh axis runs over, the one named last changes fastest.
Arguments:
- top_adj: float32 [16, 32, 16, 256], P('rhs', 'dev'), may hold values from -6 to 6
- level1_adj: float32 [16, 16, 64, 128], P('rhs', 'dev'), may hold values from -6 to 6
- image_offsets: int32 [64, 2], P('rhs'), may hold values from -6 to 6
- image_weights: float32 [64], P('rhs'), may hold values from 0.2 to 1
- incidence: float32 [16, 2], replicated, may hold values from -0.6 to 0.6
- child_list: int32 [16, 4], replicated, may hold values from 0 to 63, as said below
- theta_index_top: int32 [128, 3], replicated, may hold values from 0 to 63
- theta_weight_top: float32 [128, 3], replicated, may hold values from -2.7 to 2.7
- phi_weight_top: float32 [32, 3], replicated, may hold values from -2.7 to 2.7
- theta_index_mid: int32 [64, 3], replicated, may hold values from 0 to 31
- theta_weight_mid: float32 [64, 3], replicated, may hold values from -2.7 to 2.7
- phi_weight_mid: float32 [16, 3], replicated, may hold values from -2.7 to 2.7
Outputs:
- level0_adj: float32 [16, 256, 512], P('rhs', 'dev')
Inputs may be any that keep to these rules, and one draw needn't show every extreme that they name: `child_list`: row b holds the middle-level boxes 4 b to 4 b + 3, each once.
All inputs are finite; a program needn't handle non-finite values.
Results may differ from a plain program's by a relative error of at most 0.0003.
Values sent between devices are 32-bit elements; how exact they have to be, the bound alone decides.
No kernel may reach another device: no remote copies, remote signals or barrier semaphores. Data moves between devices by JAX's collectives and lax.ppermute only.
A program may use at most 128 MiB of HBM per device.

v0:
```python
import math
import jax
import jax.numpy as jnp
from jax import lax
from jax.sharding import PartitionSpec as P

PHASE_TOP = 18.85
PHASE_MID = 9.42
LATTICE = 12.57


def padded_2(cells, sides, width):
    for axis, dim in sides:
        count = lax.axis_size(axis)
        head = lax.slice_in_dim(cells, 0, width, axis=dim)
        tail = lax.slice_in_dim(cells, cells.shape[dim] - width, cells.shape[dim], axis=dim)
        cells = jnp.concatenate(
            [
                lax.ppermute(tail, axis, [(i, (i + 1) % count) for i in range(count)]),
                cells,
                lax.ppermute(head, axis, [((i + 1) % count, i) for i in range(count)]),
            ],
            axis=dim,
        )
    return cells


def directions(theta_count, phi_ids, phi_count):
    theta = math.pi / theta_count * (jnp.arange(theta_count, dtype=jnp.float32) + 0.5)
    azimuth = 2.0 * math.pi / phi_count * phi_ids.astype(jnp.float32)
    sin_theta = jnp.sin(theta)
    along_x = jnp.cos(azimuth)[:, None] * sin_theta[None, :]
    along_y = jnp.sin(azimuth)[:, None] * sin_theta[None, :]
    along_z = jnp.cos(theta)
    return (along_x, along_y, along_z)


def theta_matrix(index, weight, columns):
    hits = (index[:, :, None] == jnp.arange(columns, dtype=jnp.int32)[None, None, :]).astype(
        jnp.float32
    )
    return jnp.sum(weight[:, :, None] * hits, axis=1)


def phi_matrix(weight, row_ids, coarse_count, column_ids):
    target = (row_ids[:, None] // 2 + jnp.arange(3, dtype=jnp.int32)[None, :] - 1) % coarse_count
    hits = (target[:, :, None] == column_ids[None, None, :]).astype(jnp.float32)
    return jnp.sum(weight[:, :, None] * hits, axis=1)


def octant_phase(factor, octant, along_x, along_y, along_z):
    sign_x = 2.0 * (octant % 2) - 1.0
    sign_y = 2.0 * (octant // 2) - 1.0
    angle = factor * (sign_x * along_x + sign_y * along_y - along_z[None, :])
    return (jnp.cos(angle), jnp.sin(angle))


def lattice_sum(offsets, weighted, incident, along_x, along_y):
    phase_arg = LATTICE * (
        offsets[:, 0, None, None, None] * (along_x[None, None] - incident[None, :, 0, None, None])
        + offsets[:, 1, None, None, None] * (along_y[None, None] - incident[None, :, 1, None, None])
    )
    sum_real = jnp.sum(weighted[:, None, None, None] * jnp.cos(phase_arg), axis=0)
    sum_imag = jnp.sum(weighted[:, None, None, None] * jnp.sin(phase_arg), axis=0)
    return (sum_real, sum_imag)


def upper_level(
    top_real, top_imag, along_x, along_y, along_z, theta_map, phi_map, children, top_ids
):
    summed = None
    for octant in range(4):
        cosine, sine = octant_phase(PHASE_TOP, octant, along_x, along_y, along_z)
        cosine = cosine[:, None, :]
        sine = sine[:, None, :]
        stacked = jnp.stack(
            [top_real * cosine - top_imag * sine, top_real * sine + top_imag * cosine]
        )
        theta_done = jnp.einsum(
            "...pbt,tu->...pbu", stacked, theta_map, precision=lax.Precision.HIGHEST
        )
        phi_done = jnp.einsum(
            "...pbu,pq->...qbu", theta_done, phi_map, precision=lax.Precision.HIGHEST
        )
        select_map = (
            children[:, octant][:, None] - 4 * top_ids[:, None]
            == jnp.arange(4, dtype=jnp.int32)[None, :]
        ).astype(jnp.float32)
        placed = phi_done[..., None, :] * select_map[:, :, None]
        summed = placed if summed is None else summed + placed
    merged = summed.reshape(summed.shape[:-3] + (summed.shape[-3] * 4, summed.shape[-1]))
    return jnp.concatenate([merged[0], merged[1]], axis=-1)


def lower_level(middle, along_x, along_y, along_z, theta_map, phi_map):
    half_width = middle.shape[-1] // 2
    mid_real = middle[..., :half_width]
    mid_imag = middle[..., half_width:]
    real_parts = []
    imag_parts = []
    for octant in range(4):
        cosine, sine = octant_phase(PHASE_MID, octant, along_x, along_y, along_z)
        cosine = cosine[:, None, :]
        sine = sine[:, None, :]
        real_parts.append(mid_real * cosine - mid_imag * sine)
        imag_parts.append(mid_real * sine + mid_imag * cosine)
    stacked = jnp.stack([jnp.stack(real_parts, axis=-2), jnp.stack(imag_parts, axis=-2)])
    theta_done = jnp.einsum(
        "...pijt,tu->...piju", stacked, theta_map, precision=lax.Precision.HIGHEST
    )
    phi_done = jnp.einsum(
        "c...piju,pq->...ijqcu", theta_done, phi_map, precision=lax.Precision.HIGHEST
    )
    result_shape = phi_done.shape
    return phi_done.reshape(
        result_shape[:-5]
        + (result_shape[-5] * 4, result_shape[-3] * result_shape[-2] * result_shape[-1])
    )


def local(
    top_adj,
    level1_adj,
    image_offsets,
    image_weights,
    incidence,
    child_list,
    theta_index_top,
    theta_weight_top,
    phi_weight_top,
    theta_index_mid,
    theta_weight_mid,
    phi_weight_mid,
):
    dev_count = lax.axis_size("dev")
    dev_index = lax.axis_index("dev")
    rhs_count = lax.axis_size("rhs")
    exc_local, phi_local, top_boxes, top_width = top_adj.shape
    theta_top_count = top_width // 2
    theta_mid_count = theta_top_count // 2
    theta_low_count = theta_top_count // 4
    phi_top_count = phi_local * dev_count
    phi_mid_count = phi_top_count // 2
    phi_low_count = phi_top_count // 4
    image_total = image_offsets.shape[0] * rhs_count
    own_phi = dev_index * phi_local + jnp.arange(phi_local, dtype=jnp.int32)
    own_x, own_y, top_z = directions(theta_top_count, own_phi, phi_top_count)
    scaled = image_weights * float(image_total) ** (-0.5)
    part_real, part_imag = lattice_sum(
        image_offsets.astype(jnp.float32), scaled, incidence, own_x, own_y
    )
    sum_real, sum_imag = (
        lax.psum_scatter(part_real, "rhs", scatter_dimension=0, tiled=True),
        lax.psum_scatter(part_imag, "rhs", scatter_dimension=0, tiled=True),
    )
    sum_real = sum_real[:, :, None, :]
    sum_imag = sum_imag[:, :, None, :]
    top_real = top_adj[..., :theta_top_count]
    top_imag = top_adj[..., theta_top_count:]
    shifted = jnp.concatenate(
        [sum_real * top_real + sum_imag * top_imag, sum_real * top_imag - sum_imag * top_real],
        axis=-1,
    )
    theta_top = theta_matrix(theta_index_top, theta_weight_top, theta_mid_count)
    mid_all = jnp.arange(phi_mid_count, dtype=jnp.int32)
    mid_x, mid_y, mid_z = directions(theta_mid_count, mid_all, phi_mid_count)
    theta_mid = theta_matrix(theta_index_mid, theta_weight_mid, theta_low_count)
    phi_mid = phi_matrix(
        phi_weight_mid, mid_all, phi_low_count, jnp.arange(phi_low_count, dtype=jnp.int32)
    )
    padded = padded_2(shifted, (("dev", 1),), 2)
    padded_phi = (
        dev_index * phi_local - 2 + jnp.arange(phi_local + 4, dtype=jnp.int32)
    ) % phi_top_count
    pad_dirs = directions(theta_top_count, padded_phi, phi_top_count)
    picker = (padded_phi[:, None] == jnp.arange(phi_top_count, dtype=jnp.int32)[None, :]).astype(
        jnp.float32
    )
    pad_weight = jnp.dot(
        picker, phi_weight_top, precision=lax.Precision.HIGHEST, preferred_element_type=jnp.float32
    )
    own_mid = dev_index * (phi_local // 2) + jnp.arange(phi_local // 2, dtype=jnp.int32)
    phi_top = phi_matrix(pad_weight, padded_phi, phi_mid_count, own_mid)
    above = upper_level(
        padded[..., :theta_top_count],
        padded[..., theta_top_count:],
        pad_dirs[0],
        pad_dirs[1],
        top_z,
        theta_top,
        phi_top,
        child_list,
        jnp.arange(top_boxes, dtype=jnp.int32),
    )
    total = level1_adj + above
    return lower_level(
        lax.all_to_all(total, "dev", split_axis=2, concat_axis=1, tiled=True),
        mid_x,
        mid_y,
        mid_z,
        theta_mid,
        phi_mid,
    )


def solution(mesh):
    placed = (
        P("rhs", "dev", None, None),
        P("rhs", "dev", None, None),
        P("rhs", None),
        P("rhs"),
        P(),
        P(),
        P(),
        P(),
        P(),
        P(),
        P(),
        P(),
    )
    return jax.shard_map(
        local, mesh=mesh, in_specs=placed, out_specs=P("rhs", "dev", None), check_vma=False
    )
```

profile of v0, /device:TPU:0, one launch (start us, length us, event | category | flops | bytes accessed | tf_op | source)
XLA Modules:
  0.0 58.5 jit_solution(9289653000353431672)
XLA Ops:
  0.2 0.8 %slice_bitcast_fusion.2 = (f32[16]{0:T(128)S(1)}, f32[16]{0:T(128)S(1)}) fusion(f32[16,2]{0,1:T(2,128)} %param.16), kind=kLoop, calls=%fused_computation.166 | loop fusion | bytes 256 | tf_op jit(solution)/shard_map/sub | solution.py:60
  0.9 0.7 %convert_element_type.96 = f32[32,2]{0,1:T(2,128)S(1)} convert(s32[32,2]{0,1:T(2,128)} %param.14) | non-fusion elementwise | flops 64 | bytes 512 | tf_op jit(solution)/shard_map/convert_element_type | solution.py:150
  1.6 0.7 %broadcast_multiply_fusion.2 = f32[32]{0:T(128)S(1)} fusion(f32[32]{0:T(128)} %param.15), kind=kLoop, calls=%fused_computation.180 | loop fusion | flops 32 | bytes 256 | tf_op jit(solution)/shard_map/mul | solution.py:148
  2.3 0.1 broadcast_multiply_fusion.1
  2.3 0.1 broadcast_subtract_fusion
  2.4 2.3 %multiply_reduce_fusion.1 = (f32[16,2,128]{2,0,1:T(8,128)S(1)}, f32[16,2,128]{2,0,1:T(8,128)S(1)}) fusion(f32[16,2,128]{2,0,1:T(8,128)S(1)} %get-tuple-element.71, f32[32]{0:T(128)S(1)} %get-tuple-element.62, f32[16,2,128]{2,0,1:T(8,128)S(1)} %get-tuple-element.72, f32[32]{0:T(128)S(1)} %get-tuple-element.61, f32[32]{0:T(128)S(1)} %broadcast_multiply_fusion.2), kind=kLoop, calls=%fused_computation.36 | loop fusion | flops 1040384 | bytes 65920 | tf_op jit(solution)/shard_map/reduce_sum | solution.py:63
  4.8 9.9 %all-reduce.2 = (f32[16,2,128]{2,1,0:T(2,128)S(1)}, f32[16,2,128]{2,1,0:T(2,128)S(1)}) all-reduce(f32[16,2,128]{2,1,0:T(2,128)S(1)} %copy.63, f32[16,2,128]{2,1,0:T(2,128)S(1)} %copy.62), channel_id=3, replica_groups=mesh['dev'=16,'rhs'=2] {'rhs'}, use_global_device_ids=true, to_apply=%region_5.0.clone | all-reduce | flops 8192 | bytes 65536
  14.8 1.2 %dynamic-slice = u32[1]{0:T(128)} dynamic-slice(u32[32]{0:T(128)} %constant.115, u32[]{:T(128)S(6)} %add.397), dynamic_slice_sizes={1} | dynamic-slice | bytes 12
  16.7 1.0 %multiply_add_fusion.1 = (f32[8,2,16,128]{3,2,1,0:T(8,128)S(1)}, f32[8,2,16,128]{3,2,1,0:T(8,128)S(1)}) fusion(f32[8,2,16,256]{3,2,1,0:T(8,128)} %param.12, f32[8,2,128]{2,1,0:T(2,128)S(1)} %constant_dynamic-slice_fusion, f32[8,2,128]{2,1,0:T(2,128)S(1)} %constant_dynamic-slice_fusion.1), kind=kLoop, calls=%fused_computation.58 | loop fusion | flops 196608 | bytes 540672 | tf_op jit(solution)/shard_map/add | solution.py:161
  17.7 0.1 collective-permute-start
  17.8 4.4 %collective-permute-start.1 = (f32[8,2,16,256]{3,2,1,0:T(8,128)S(1)}, f32[8,2,16,256]{3,2,1,0:T(8,128)S(1)}, u32[]{:S(2)}, u32[]{:S(2)}) collective-permute-start(f32[8,2,16,256]{3,2,1,0:T(8,128)S(1)} %pad_maximum_fusion.1), channel_id=1, source_target_pairs={{2,0},{4,2},{6,4},{8,6},{10,8},{12,10},{14,12},{16,14},{18,16},{20... | collective-permute-start | bytes 786440 | tf_op jit(solution)/shard_map/ppermute | solution.py:21
  22.2 0.1 fusion.90
  22.3 0.8 %subtract_bitcast_fusion.11 = (s32[16]{0:T(128)S(1)}, s32[16]{0:T(128)S(1)}, s32[16]{0:T(128)S(1)}, s32[16]{0:T(128)S(1)}) fusion(s32[16,4]{0,1:T(4,128)} %param.17), kind=kLoop, calls=%fused_computation.161 | loop fusion | flops 80 | bytes 512 | tf_op jit(solution)/shard_map/eq | solution.py:86
  23.2 0.7 %select_reduce_fusion = f32[128,64]{0,1:T(8,128)S(1)} fusion(f32[128,3]{0,1:T(4,128)} %param.19, s32[128,3]{0,1:T(4,128)} %param.18), kind=kLoop, calls=%fused_computation.59 | loop fusion | flops 65536 | bytes 35840 | tf_op jit(solution)/shard_map/reduce_sum | solution.py:42
  23.9 0.1 fusion.51
  24.0 0.1 fusion.53
  24.1 0.2 fusion.4
  24.3 0.1 fusion.59
  24.5 1.9 %collective-permute-done = f32[8,2,16,256]{3,2,1,0:T(8,128)S(1)} collective-permute-done((f32[8,2,16,256]{3,2,1,0:T(8,128)S(1)}, f32[8,2,16,256]{3,2,1,0:T(8,128)S(1)}, u32[]{:S(2)}, u32[]{:S(2)}) %collective-permute-start) | collective-permute-done | bytes 262176 | tf_op jit(solution)/shard_map/ppermute | solution.py:19
  26.4 0.0 collective-permute-done.1
  26.4 0.1 pad_maximum_fusion
  26.4 0.3 subtract_bitcast_fusion.3
  26.8 0.8 %fusion.13 = f32[2,8,6,16,64]{4,3,2,1,0:T(8,128)S(1)} fusion(f32[1,8,6,16,128]{4,3,2,1,0:T(8,128)S(1)} %get-tuple-element.10, f32[1,8,6,16,128]{4,3,2,1,0:T(8,128)S(1)} %get-tuple-element.9, f32[128,64]{0,1:T(8,128)S(1)} %select_reduce_fusion), kind=kOutput, calls=%fused_computation.18 | convolution fusion | flops 151191552 | bytes 1212416 | tf_op jit(solution)/shard_map/...pbt,tu->...pbu/dot_general | solution.py:79
  27.6 1.1 %fusion.11 = f32[1,2,8,16,64]{4,0,3,2,1:T(1,128)S(1)} fusion(f32[2,8,6,16,64]{4,3,2,1,0:T(8,128)S(1)} %fusion.13, f32[6]{0:T(128)S(1)} %fusion.4), kind=kOutput, calls=%fused_computation.15 | convolution fusion | flops 1179648 | bytes 458776 | tf_op jit(solution)/shard_map/...pbu,pq->...qbu/dot_general | solution.py:82
  28.7 0.8 %fusion.17 = f32[2,8,6,16,64]{4,3,2,1,0:T(8,128)S(1)} fusion(f32[1,8,6,16,128]{4,3,2,1,0:T(8,128)S(1)} %get-tuple-element.17, f32[1,8,6,16,128]{4,3,2,1,0:T(8,128)S(1)} %get-tuple-element.18, f32[128,64]{0,1:T(8,128)S(1)} %select_reduce_fusion), kind=kOutput, calls=%fused_computation.22 | convolution fusion | flops 151191552 | bytes 1212416 | tf_op jit(solution)/shard_map/...pbt,tu->...pbu/dot_general | solution.py:79
  29.5 1.1 %fusion.9 = f32[1,2,8,16,64]{4,0,3,2,1:T(1,128)S(1)} fusion(f32[2,8,6,16,64]{4,3,2,1,0:T(8,128)S(1)} %fusion.17, f32[6]{0:T(128)S(1)} %fusion.4), kind=kOutput, calls=%fused_computation.13 | convolution fusion | flops 1179648 | bytes 458776 | tf_op jit(solution)/shard_map/...pbu,pq->...qbu/dot_general | solution.py:82
  30.6 0.8 %fusion.21 = f32[2,8,6,16,64]{4,3,2,1,0:T(8,128)S(1)} fusion(f32[1,8,6,16,128]{4,3,2,1,0:T(8,128)S(1)} %get-tuple-element.19, f32[1,8,6,16,128]{4,3,2,1,0:T(8,128)S(1)} %get-tuple-element.20, f32[128,64]{0,1:T(8,128)S(1)} %select_reduce_fusion), kind=kOutput, calls=%fused_computation.26 | convolution fusion | flops 151191552 | bytes 1212416 | tf_op jit(solution)/shard_map/...pbt,tu->...pbu/dot_general | solution.py:79
  31.4 1.1 %fusion.7 = f32[1,2,8,16,64]{4,0,3,2,1:T(1,128)S(1)} fusion(f32[2,8,6,16,64]{4,3,2,1,0:T(8,128)S(1)} %fusion.21, f32[6]{0:T(128)S(1)} %fusion.4), kind=kOutput, calls=%fused_computation.11 | convolution fusion | flops 1179648 | bytes 458776 | tf_op jit(solution)/shard_map/...pbu,pq->...qbu/dot_general | solution.py:82
  32.6 0.1 subtract_bitcast_fusion
  32.7 0.8 %fusion.25 = f32[2,8,6,16,64]{4,3,2,1,0:T(8,128)S(1)} fusion(f32[1,8,6,16,128]{4,3,2,1,0:T(8,128)S(1)} %get-tuple-element.16, f32[1,8,6,16,128]{4,3,2,1,0:T(8,128)S(1)} %get-tuple-element.15, f32[128,64]{0,1:T(8,128)S(1)} %select_reduce_fusion), kind=kOutput, calls=%fused_computation.30 | convolution fusion | flops 151191552 | bytes 1212416 | tf_op jit(solution)/shard_map/...pbt,tu->...pbu/dot_general | solution.py:79
  33.4 0.0 copy-start.1
  33.5 1.1 %fusion.5 = f32[1,2,8,16,64]{4,0,3,2,1:T(1,128)S(1)} fusion(f32[2,8,6,16,64]{4,3,2,1,0:T(8,128)S(1)} %fusion.25, f32[6]{0:T(128)S(1)} %fusion.4), kind=kOutput, calls=%fused_computation.9 | convolution fusion | flops 1179648 | bytes 458776 | tf_op jit(solution)/shard_map/...pbu,pq->...qbu/dot_general | solution.py:82
  34.6 0.0 copy-start.4
  34.6 0.0 copy-start.2
  34.6 0.0 copy-start.3
  34.6 0.4 multiply_add_fusion
  35.1 0.1 pad_maximum_fusion.2
  35.3 1.0 %copy_add_fusion = f32[8,1,64,128]{3,0,1,2:T(8,128)} fusion(f32[8,1,64,128]{3,2,1,0:T(8,128)S(1)} %pad_maximum_fusion.2, f32[8,1,64,128]{3,2,1,0:T(8,128)S(1)} %copy-done.1), kind=kLoop, calls=%fused_computation.48 | loop fusion | flops 65536 | bytes 786432 | tf_op jit(solution)/shard_map/add | solution.py:195
  36.2 5.7 %all-to-all-start = ((f32[8,1,64,128]{3,0,1,2:T(8,128)}), f32[8,1,64,128]{3,0,1,2:T(8,128)S(1)}, u32[]{:S(2)}, u32[]{:S(2)}) async-start(f32[8,1,64,128]{3,0,1,2:T(8,128)} %copy_add_fusion), calls=%async_computation | async-start | bytes 524288 | tf_op jit(solution)/shard_map/all_to_all | solution.py:197
  42.1 0.2 fusion.38
  42.3 9.7 %all-to-all-done = f32[8,1,64,128]{3,0,1,2:T(8,128)S(1)} async-done(((f32[8,1,64,128]{3,0,1,2:T(8,128)}), f32[8,1,64,128]{3,0,1,2:T(8,128)S(1)}, u32[]{:S(2)}, u32[]{:S(2)}) %all-to-all-start) | async-done | bytes 262176 | tf_op jit(solution)/shard_map/all_to_all | solution.py:197
  52.0 0.1 fusion.98
  52.1 0.4 subtract_bitcast_fusion.7
  52.5 0.1 maximum_bitcast_fusion.1
  52.7 1.8 %fusion = f32[2,8,16,4,4,32]{5,2,4,3,1,0:T(8,128)S(1)} fusion(f32[1,8,16,4,4,64]{5,2,4,3,1,0:T(8,128)S(1)} %maximum_bitcast_fusion.1, f32[64,32]{0,1:T(8,128)S(1)} %select_reduce_fusion.1, f32[8,16,4,1,64]{4,1,2,0,3:T(8,128)S(1)} %get-tuple-element.34, f32[8,16,4,1,64]{4,1,2,0,3:T(8,128)S(1)} %get-tuple-element.32, ...), kind=kOutput, calls=%fused_computation | convolution fusion | flops 101318656 | bytes 1581056 | tf_op jit(solution)/shard_map/...pijt,tu->...piju/dot_general | solution.py:108
  54.4 1.1 %convolution_bitcast_fusion = f32[8,4,4,8,2,32]{5,3,2,1,0,4:T(8,128)S(1)} fusion(f32[2,8,16,4,4,32]{5,2,4,3,1,0:T(8,128)S(1)} %fusion, f32[16,8]{0,1:T(8,128)S(1)} %select_reduce_fusion.2), kind=kOutput, calls=%fused_computation.4 | convolution fusion | flops 12582912 | bytes 786944 | tf_op jit(solution)/shard_map/c...piju,pq->...ijqcu/dot_general | solution.py:111
  55.6 0.8 %copy.72 = f32[8,4,4,8,2,32]{5,4,3,2,1,0:T(2,128)S(1)} copy(f32[8,4,4,8,2,32]{5,3,2,1,0,4:T(8,128)S(1)} %convolution_bitcast_fusion) | data formatting | bytes 524288 | tf_op jit(solution)/shard_map/c...piju,pq->...ijqcu/transpose | solution.py:111
  56.4 2.1 %reshape.1499 = f32[8,16,512]{2,1,0:T(8,128)} reshape(f32[8,4,4,8,2,32]{5,4,3,2,1,0:T(2,128)S(1)} %copy.72) | data formatting | bytes 524288 | tf_op jit(solution)/shard_map/reshape | solution.py:115
  (24 shorter events, 0.4 us)
Async XLA Ops:
  0.0 24.1 %copy-start = (f32[32,3]{0,1:T(4,128)S(1)}, f32[32,3]{0,1:T(4,128)}, u32[]{:S(2)}) copy-start(f32[32,3]{0,1:T(4,128)} %param.20) | copy-start | bytes 1156
  17.7 8.6 %collective-permute-start = (f32[8,2,16,256]{3,2,1,0:T(8,128)S(1)}, f32[8,2,16,256]{3,2,1,0:T(8,128)S(1)}, u32[]{:S(2)}, u32[]{:S(2)}) collective-permute-start(f32[8,2,16,256]{3,2,1,0:T(8,128)S(1)} %pad_maximum_fusion.1), channel_id=1, source_target_pairs={{0,2},{2,4},{4,6},{6,8},{8,10},{10,12},{12,14},{14,16},{16,18},{18... | collective-permute-start | bytes 786440 | tf_op jit(solution)/shard_map/ppermute | solution.py:19
  17.8 8.6 %collective-permute-start.1 = (f32[8,2,16,256]{3,2,1,0:T(8,128)S(1)}, f32[8,2,16,256]{3,2,1,0:T(8,128)S(1)}, u32[]{:S(2)}, u32[]{:S(2)}) collective-permute-start(f32[8,2,16,256]{3,2,1,0:T(8,128)S(1)} %pad_maximum_fusion.1), channel_id=1, source_target_pairs={{2,0},{4,2},{6,4},{8,6},{10,8},{12,10},{14,12},{16,14},{18,16},{20... | collective-permute-start | bytes 786440 | tf_op jit(solution)/shard_map/ppermute | solution.py:21
  33.4 1.8 %copy-start.1 = (f32[8,1,64,128]{3,2,1,0:T(8,128)S(1)}, f32[8,1,64,128]{3,2,1,0:T(8,128)}, u32[]{:S(2)}) copy-start(f32[8,1,64,128]{3,2,1,0:T(8,128)} %param.13) | copy-start | bytes 786436
  34.6 7.4 %copy-start.4 = (f32[16,3]{0,1:T(4,128)S(1)}, f32[16,3]{0,1:T(4,128)}, u32[]{:S(2)}) copy-start(f32[16,3]{0,1:T(4,128)} %param.23) | copy-start | bytes 580
  34.6 7.4 %copy-start.2 = (f32[64,3]{0,1:T(4,128)S(1)}, f32[64,3]{0,1:T(4,128)}, u32[]{:S(2)}) copy-start(f32[64,3]{0,1:T(4,128)} %param.22) | copy-start | bytes 2308
  34.6 7.4 %copy-start.3 = (s32[64,3]{0,1:T(4,128)S(1)}, s32[64,3]{0,1:T(4,128)}, u32[]{:S(2)}) copy-start(s32[64,3]{0,1:T(4,128)} %param.21) | copy-start | bytes 2308
  36.2 15.7 %all-to-all-start = ((f32[8,1,64,128]{3,0,1,2:T(8,128)}), f32[8,1,64,128]{3,0,1,2:T(8,128)S(1)}, u32[]{:S(2)}, u32[]{:S(2)}) async-start(f32[8,1,64,128]{3,0,1,2:T(8,128)} %copy_add_fusion), calls=%async_computation | async-start | bytes 524288 | tf_op jit(solution)/shard_map/all_to_all | solution.py:197
where the time goes:
time: 58.9 us; the launch traced here: 58.5 us
  waiting for transfers between devices  11.6 us (20%)
  matrix products  10.7 us (18%)
  starting transfers between devices  10.2 us (17%)
  blocking collectives  9.94 us (17%)
  other arithmetic  9.84 us (17%)
  local copies, waits for them, and re-layouts  5.15 us (9%)
  between operations  1.03 us (2%)
    unnamed x1, blocking collectives  9.94 us
    all_to_all x1, waiting for transfers between devices, local(): lax.all_to_all(total, 'dev', split_axis=2, concat_axis=1, tiled=True)  9.69 us
    all_to_all x1, starting transfers between devices, local(): lax.all_to_all(total, 'dev', split_axis=2, concat_axis=1, tiled=True)  5.73 us
    dot_general x4, matrix products, upper_level(): jnp.einsum('...pbu,pq->...qbu', theta_done, phi_map, precision=lax.Precis...  4.54 us
    ppermute x1, starting transfers between devices, padded_2(): lax.ppermute(head, axis, [((i + 1) % count, i) for i in range(count)])  4.43 us
    dot_general x4, matrix products, upper_level(): jnp.einsum('...pbt,tu->...pbu', stacked, theta_map, precision=lax.Precisi...  3.09 us
    reduce_sum x1, other arithmetic, lattice_sum(): jnp.sum(weighted[:, None, None, None] * jnp.cos(phase_arg), axis=0)  2.35 us
    reshape x1, local copies, waits for them, and re-layouts, lower_level(): phi_done.reshape(result_shape[:-5] + (result_shape[-5] * 4, result_shape[...  2.08 us
  transfers between devices with their start and end apart: 3, of which 2 were waited for; matrix products, arithmetic and copies ran while one was open for 4% of the time, Pallas kernels for 0%

commit v1 on v0

--- a/solution.py
+++ b/solution.py
@@ -194,7 +194,10 @@
     )
     total = level1_adj + above
     return lower_level(
-        lax.all_to_all(total, "dev", split_axis=2, concat_axis=1, tiled=True),
+        jnp.concatenate(
+            lax.all_to_all(jnp.stack(jnp.split(total, lax.axis_size("dev"), axis=2)), "dev", 0, 0),
+            axis=1,
+        ),
         mid_x,
         mid_y,
         mid_z,

time: 58.9 us -> 67.8 us (1.15)
  local copies, waits for them, and re-layouts: 5.15 us -> 14.9 us
  other arithmetic: 9.84 us -> 8.93 us
    unnamed x13 -> x28, local copies, waits for them, and re-layouts: 1.29 us -> 10.4 us
    add x1, other arithmetic: 1 us -> 0.14 us  [local(): total = level1_adj + above]
where the time goes in v1:
time: 67.8 us; the launch traced here: 67.4 us
  local copies, waits for them, and re-layouts  14.9 us (22%)
  waiting for transfers between devices  11.6 us (17%)
  matrix products  10.7 us (16%)
  starting transfers between devices  10.2 us (15%)
  blocking collectives  9.94 us (15%)
  other arithmetic  8.93 us (13%)
  between operations  1.04 us (2%)
    unnamed x28, local copies, waits for them, and re-layouts  10.4 us
    unnamed x1, blocking collectives  9.94 us
    all_to_all x1, waiting for transfers between devices, local(): lax.all_to_all(jnp.stack(jnp.split(total, lax.axis_size('dev'), axis=2)),...  9.69 us
    all_to_all x1, starting transfers between devices, local(): lax.all_to_all(jnp.stack(jnp.split(total, lax.axis_size('dev'), axis=2)),...  5.73 us
    dot_general x4, matrix products, upper_level(): jnp.einsum('...pbu,pq->...qbu', theta_done, phi_map, precision=lax.Precis...  4.54 us
    ppermute x1, starting transfers between devices, padded_2(): lax.ppermute(head, axis, [((i + 1) % count, i) for i in range(count)])  4.43 us
    dot_general x4, matrix products, upper_level(): jnp.einsum('...pbt,tu->...pbu', stacked, theta_map, precision=lax.Precisi...  3.08 us
    reduce_sum x1, other arithmetic, lattice_sum(): jnp.sum(weighted[:, None, None, None] * jnp.cos(phase_arg), axis=0)  2.35 us
  transfers between devices with their start and end apart: 3, of which 2 were waited for; matrix products, arithmetic and copies ran while one was open for 4% of the time, Pallas kernels for 0%

profile of v1, /device:TPU:0, one launch (start us, length us, event | category | flops | bytes accessed | tf_op | source)
XLA Modules:
  0.0 67.4 jit_solution(13956764866630584606)
XLA Ops:
  0.2 0.8 %slice_bitcast_fusion.18 = (f32[16]{0:T(128)S(1)}, f32[16]{0:T(128)S(1)}) fusion(f32[16,2]{0,1:T(2,128)} %param.16), kind=kLoop, calls=%fused_computation.198 | loop fusion | bytes 256 | tf_op jit(solution)/shard_map/sub | solution.py:60
  0.9 0.7 %convert_element_type.96 = f32[32,2]{0,1:T(2,128)S(1)} convert(s32[32,2]{0,1:T(2,128)} %param.14) | non-fusion elementwise | flops 64 | bytes 512 | tf_op jit(solution)/shard_map/convert_element_type | solution.py:150
  1.6 0.7 broadcast_multiply_fusion.2
  2.4 2.3 %multiply_reduce_fusion.1 = (f32[16,2,128]{2,0,1:T(8,128)S(1)}, f32[16,2,128]{2,0,1:T(8,128)S(1)}) fusion(f32[16,2,128]{2,0,1:T(8,128)S(1)} %get-tuple-element.67, f32[32]{0:T(128)S(1)} %get-tuple-element.58, f32[16,2,128]{2,0,1:T(8,128)S(1)} %get-tuple-element.68, f32[32]{0:T(128)S(1)} %get-tuple-element.57, f32[32]{0:T(128)S(1)} %broadcast_multiply_fusion.2), kind=kLoop, calls=%fused_computation.36 | loop fusion | flops 1040384 | bytes 65920 | tf_op jit(solution)/shard_map/reduce_sum | solution.py:63
  4.8 9.9 %all-reduce.2 = (f32[16,2,128]{2,1,0:T(2,128)S(1)}, f32[16,2,128]{2,1,0:T(2,128)S(1)}) all-reduce(f32[16,2,128]{2,1,0:T(2,128)S(1)} %copy.93, f32[16,2,128]{2,1,0:T(2,128)S(1)} %copy.92), channel_id=3, replica_groups=mesh['dev'=16,'rhs'=2] {'rhs'}, use_global_device_ids=true, to_apply=%region_5.0.clone | all-reduce | flops 8192 | bytes 65536
  14.8 1.2 %dynamic-slice = u32[1]{0:T(128)} dynamic-slice(u32[32]{0:T(128)} %constant.115, u32[]{:T(128)S(6)} %add.397), dynamic_slice_sizes={1} | dynamic-slice | bytes 12
  16.7 1.0 %multiply_add_fusion.1 = (f32[8,2,16,128]{3,2,1,0:T(8,128)S(1)}, f32[8,2,16,128]{3,2,1,0:T(8,128)S(1)}) fusion(f32[8,2,16,256]{3,2,1,0:T(8,128)} %param.12, f32[8,2,128]{2,1,0:T(2,128)S(1)} %constant_dynamic-slice_fusion, f32[8,2,128]{2,1,0:T(2,128)S(1)} %constant_dynamic-slice_fusion.1), kind=kLoop, calls=%fused_computation.58 | loop fusion | flops 196608 | bytes 540672 | tf_op jit(solution)/shard_map/add | solution.py:161
  17.8 4.4 %collective-permute-start.1 = (f32[8,2,16,256]{3,2,1,0:T(8,128)S(1)}, f32[8,2,16,256]{3,2,1,0:T(8,128)S(1)}, u32[]{:S(2)}, u32[]{:S(2)}) collective-permute-start(f32[8,2,16,256]{3,2,1,0:T(8,128)S(1)} %pad_maximum_fusion.1), channel_id=1, source_target_pairs={{2,0},{4,2},{6,4},{8,6},{10,8},{12,10},{14,12},{16,14},{18,16},{20... | collective-permute-start | bytes 786440 | tf_op jit(solution)/shard_map/ppermute | solution.py:21
  22.3 0.8 %subtract_bitcast_fusion.11 = (s32[16]{0:T(128)S(1)}, s32[16]{0:T(128)S(1)}, s32[16]{0:T(128)S(1)}, s32[16]{0:T(128)S(1)}) fusion(s32[16,4]{0,1:T(4,128)} %param.17), kind=kLoop, calls=%fused_computation.193 | loop fusion | flops 80 | bytes 512 | tf_op jit(solution)/shard_map/eq | solution.py:86
  23.2 0.7 %select_reduce_fusion = f32[128,64]{0,1:T(8,128)S(1)} fusion(f32[128,3]{0,1:T(4,128)} %param.19, s32[128,3]{0,1:T(4,128)} %param.18), kind=kLoop, calls=%fused_computation.59 | loop fusion | flops 65536 | bytes 35840 | tf_op jit(solution)/shard_map/reduce_sum | solution.py:42
  24.1 0.2 fusion.4
  24.3 0.1 fusion.59
  24.5 1.9 %collective-permute-done = f32[8,2,16,256]{3,2,1,0:T(8,128)S(1)} collective-permute-done((f32[8,2,16,256]{3,2,1,0:T(8,128)S(1)}, f32[8,2,16,256]{3,2,1,0:T(8,128)S(1)}, u32[]{:S(2)}, u32[]{:S(2)}) %collective-permute-start) | collective-permute-done | bytes 262176 | tf_op jit(solution)/shard_map/ppermute | solution.py:19
  26.4 0.3 subtract_bitcast_fusion.3
  26.8 0.8 %fusion.13 = f32[2,8,6,16,64]{4,3,2,1,0:T(8,128)S(1)} fusion(f32[1,8,6,16,128]{4,3,2,1,0:T(8,128)S(1)} %get-tuple-element.10, f32[1,8,6,16,128]{4,3,2,1,0:T(8,128)S(1)} %get-tuple-element.9, f32[128,64]{0,1:T(8,128)S(1)} %select_reduce_fusion), kind=kOutput, calls=%fused_computation.18 | convolution fusion | flops 151191552 | bytes 1212416 | tf_op jit(solution)/shard_map/...pbt,tu->...pbu/dot_general | solution.py:79
  27.6 1.1 %fusion.11 = f32[1,2,8,16,64]{4,0,3,2,1:T(1,128)S(1)} fusion(f32[2,8,6,16,64]{4,3,2,1,0:T(8,128)S(1)} %fusion.13, f32[6]{0:T(128)S(1)} %fusion.4), kind=kOutput, calls=%fused_computation.15 | convolution fusion | flops 1179648 | bytes 458776 | tf_op jit(solution)/shard_map/...pbu,pq->...qbu/dot_general | solution.py:82
  28.7 0.8 %fusion.17 = f32[2,8,6,16,64]{4,3,2,1,0:T(8,128)S(1)} fusion(f32[1,8,6,16,128]{4,3,2,1,0:T(8,128)S(1)} %get-tuple-element.17, f32[1,8,6,16,128]{4,3,2,1,0:T(8,128)S(1)} %get-tuple-element.18, f32[128,64]{0,1:T(8,128)S(1)} %select_reduce_fusion), kind=kOutput, calls=%fused_computation.22 | convolution fusion | flops 151191552 | bytes 1212416 | tf_op jit(solution)/shard_map/...pbt,tu->...pbu/dot_general | solution.py:79
  29.5 1.1 %fusion.9 = f32[1,2,8,16,64]{4,0,3,2,1:T(1,128)S(1)} fusion(f32[2,8,6,16,64]{4,3,2,1,0:T(8,128)S(1)} %fusion.17, f32[6]{0:T(128)S(1)} %fusion.4), kind=kOutput, calls=%fused_computation.13 | convolution fusion | flops 1179648 | bytes 458776 | tf_op jit(solution)/shard_map/...pbu,pq->...qbu/dot_general | solution.py:82
  30.6 0.8 %fusion.21 = f32[2,8,6,16,64]{4,3,2,1,0:T(8,128)S(1)} fusion(f32[1,8,6,16,128]{4,3,2,1,0:T(8,128)S(1)} %get-tuple-element.19, f32[1,8,6,16,128]{4,3,2,1,0:T(8,128)S(1)} %get-tuple-element.20, f32[128,64]{0,1:T(8,128)S(1)} %select_reduce_fusion), kind=kOutput, calls=%fused_computation.26 | convolution fusion | flops 151191552 | bytes 1212416 | tf_op jit(solution)/shard_map/...pbt,tu->...pbu/dot_general | solution.py:79
  31.4 1.1 %fusion.7 = f32[1,2,8,16,64]{4,0,3,2,1:T(1,128)S(1)} fusion(f32[2,8,6,16,64]{4,3,2,1,0:T(8,128)S(1)} %fusion.21, f32[6]{0:T(128)S(1)} %fusion.4), kind=kOutput, calls=%fused_computation.11 | convolution fusion | flops 1179648 | bytes 458776 | tf_op jit(solution)/shard_map/...pbu,pq->...qbu/dot_general | solution.py:82
  32.7 0.8 %fusion.25 = f32[2,8,6,16,64]{4,3,2,1,0:T(8,128)S(1)} fusion(f32[1,8,6,16,128]{4,3,2,1,0:T(8,128)S(1)} %get-tuple-element.16, f32[1,8,6,16,128]{4,3,2,1,0:T(8,128)S(1)} %get-tuple-element.15, f32[128,64]{0,1:T(8,128)S(1)} %select_reduce_fusion), kind=kOutput, calls=%fused_computation.30 | convolution fusion | flops 151191552 | bytes 1212416 | tf_op jit(solution)/shard_map/...pbt,tu->...pbu/dot_general | solution.py:79
  33.5 1.1 %fusion.5 = f32[1,2,8,16,64]{4,0,3,2,1:T(1,128)S(1)} fusion(f32[2,8,6,16,64]{4,3,2,1,0:T(8,128)S(1)} %fusion.25, f32[6]{0:T(128)S(1)} %fusion.4), kind=kOutput, calls=%fused_computation.9 | convolution fusion | flops 1179648 | bytes 458776 | tf_op jit(solution)/shard_map/...pbu,pq->...qbu/dot_general | solution.py:82
  34.6 0.4 multiply_add_fusion
  35.2 0.6 constant_dynamic-update-slice_fusion.15
  35.9 0.6 constant_dynamic-update-slice_fusion.14
  36.5 0.6 constant_dynamic-update-slice_fusion.13
  37.1 0.6 constant_dynamic-update-slice_fusion.12
  37.7 0.6 constant_dynamic-update-slice_fusion.11
  38.3 0.6 constant_dynamic-update-slice_fusion.10
  38.9 0.6 constant_dynamic-update-slice_fusion.9
  39.5 0.6 constant_dynamic-update-slice_fusion.8
  40.1 0.6 constant_dynamic-update-slice_fusion.7
  40.7 0.6 constant_dynamic-update-slice_fusion.6
  41.4 0.6 constant_dynamic-update-slice_fusion.5
  42.0 0.6 constant_dynamic-update-slice_fusion.4
  42.6 0.6 constant_dynamic-update-slice_fusion.3
  43.2 0.6 constant_dynamic-update-slice_fusion.2
  43.8 0.6 constant_dynamic-update-slice_fusion.1
  44.4 0.6 constant_dynamic-update-slice_fusion
  45.0 5.7 %all-to-all-start = ((f32[16,8,1,4,128]{4,3,1,2,0:T(4,128)}), f32[16,8,1,4,128]{4,3,1,2,0:T(4,128)S(1)}, u32[]{:S(2)}, u32[]{:S(2)}) async-start(f32[16,8,1,4,128]{4,3,1,2,0:T(4,128)} %constant_dynamic-update-slice_fusion), calls=%async_computation | async-start | bytes 524288 | tf_op jit(solution)/shard_map/all_to_all | solution.py:198
  50.9 0.2 fusion.38
  51.1 9.7 %all-to-all-done = f32[16,8,1,4,128]{4,3,1,2,0:T(4,128)S(1)} async-done(((f32[16,8,1,4,128]{4,3,1,2,0:T(4,128)}), f32[16,8,1,4,128]{4,3,1,2,0:T(4,128)S(1)}, u32[]{:S(2)}, u32[]{:S(2)}) %all-to-all-start) | async-done | bytes 262176 | tf_op jit(solution)/shard_map/all_to_all | solution.py:198
  60.8 0.2 copy.128
  61.1 0.4 subtract_bitcast_fusion.7
  61.6 1.8 %fusion = f32[2,8,16,4,4,32]{5,2,4,3,1,0:T(8,128)S(1)} fusion(f32[1,8,16,4,4,64]{5,2,4,3,1,0:T(8,128)S(1)} %maximum_bitcast_fusion.1, f32[64,32]{0,1:T(8,128)S(1)} %select_reduce_fusion.1, f32[8,16,4,1,64]{4,1,2,0,3:T(8,128)S(1)} %get-tuple-element.36, f32[8,16,4,1,64]{4,1,2,0,3:T(8,128)S(1)} %get-tuple-element.34, ...), kind=kOutput, calls=%fused_computation | convolution fusion | flops 101318656 | bytes 1581056 | tf_op jit(solution)/shard_map/...pijt,tu->...piju/dot_general | solution.py:108
  63.3 1.1 %convolution_bitcast_fusion = f32[8,4,4,8,2,32]{5,3,2,1,0,4:T(8,128)S(1)} fusion(f32[2,8,16,4,4,32]{5,2,4,3,1,0:T(8,128)S(1)} %fusion, f32[16,8]{0,1:T(8,128)S(1)} %select_reduce_fusion.2), kind=kOutput, calls=%fused_computation.4 | convolution fusion | flops 12582912 | bytes 786944 | tf_op jit(solution)/shard_map/c...piju,pq->...ijqcu/dot_general | solution.py:111
  64.5 0.8 %copy.100 = f32[8,4,4,8,2,32]{5,4,3,2,1,0:T(2,128)S(1)} copy(f32[8,4,4,8,2,32]{5,3,2,1,0,4:T(8,128)S(1)} %convolution_bitcast_fusion) | data formatting | bytes 524288 | tf_op jit(solution)/shard_map/c...piju,pq->...ijqcu/transpose | solution.py:111
  65.3 2.1 %reshape.1504 = f32[8,16,512]{2,1,0:T(8,128)} reshape(f32[8,4,4,8,2,32]{5,4,3,2,1,0:T(2,128)S(1)} %copy.100) | data formatting | bytes 524288 | tf_op jit(solution)/shard_map/reshape | solution.py:115
  (40 shorter events, 1.4 us)
Async XLA Ops:
  0.0 24.1 %copy-start = (f32[32,3]{0,1:T(4,128)S(1)}, f32[32,3]{0,1:T(4,128)}, u32[]{:S(2)}) copy-start(f32[32,3]{0,1:T(4,128)} %param.20) | copy-start | bytes 1156
  17.7 8.6 %collective-permute-start = (f32[8,2,16,256]{3,2,1,0:T(8,128)S(1)}, f32[8,2,16,256]{3,2,1,0:T(8,128)S(1)}, u32[]{:S(2)}, u32[]{:S(2)}) collective-permute-start(f32[8,2,16,256]{3,2,1,0:T(8,128)S(1)} %pad_maximum_fusion.1), channel_id=1, source_target_pairs={{0,2},{2,4},{4,6},{6,8},{8,10},{10,12},{12,14},{14,16},{16,18},{18... | collective-permute-start | bytes 786440 | tf_op jit(solution)/shard_map/ppermute | solution.py:19
  17.8 8.6 %collective-permute-start.1 = (f32[8,2,16,256]{3,2,1,0:T(8,128)S(1)}, f32[8,2,16,256]{3,2,1,0:T(8,128)S(1)}, u32[]{:S(2)}, u32[]{:S(2)}) collective-permute-start(f32[8,2,16,256]{3,2,1,0:T(8,128)S(1)} %pad_maximum_fusion.1), channel_id=1, source_target_pairs={{2,0},{4,2},{6,4},{8,6},{10,8},{12,10},{14,12},{16,14},{18,16},{20... | collective-permute-start | bytes 786440 | tf_op jit(solution)/shard_map/ppermute | solution.py:21
  32.7 2.4 %copy-start.1 = (f32[8,1,64,128]{3,2,1,0:T(8,128)S(1)}, f32[8,1,64,128]{3,2,1,0:T(8,128)}, u32[]{:S(2)}) copy-start(f32[8,1,64,128]{3,2,1,0:T(8,128)} %param.13) | copy-start | bytes 786436
  34.6 16.2 %copy-start.4 = (f32[16,3]{0,1:T(4,128)S(1)}, f32[16,3]{0,1:T(4,128)}, u32[]{:S(2)}) copy-start(f32[16,3]{0,1:T(4,128)} %param.23) | copy-start | bytes 580
  34.6 16.2 %copy-start.2 = (f32[64,3]{0,1:T(4,128)S(1)}, f32[64,3]{0,1:T(4,128)}, u32[]{:S(2)}) copy-start(f32[64,3]{0,1:T(4,128)} %param.22) | copy-start | bytes 2308
  34.6 16.2 %copy-start.3 = (s32[64,3]{0,1:T(4,128)S(1)}, s32[64,3]{0,1:T(4,128)}, u32[]{:S(2)}) copy-start(s32[64,3]{0,1:T(4,128)} %param.21) | copy-start | bytes 2308
  45.0 15.7 %all-to-all-start = ((f32[16,8,1,4,128]{4,3,1,2,0:T(4,128)}), f32[16,8,1,4,128]{4,3,1,2,0:T(4,128)S(1)}, u32[]{:S(2)}, u32[]{:S(2)}) async-start(f32[16,8,1,4,128]{4,3,1,2,0:T(4,128)} %constant_dynamic-update-slice_fusion), calls=%async_computation | async-start | bytes 524288 | tf_op jit(solution)/shard_map/all_to_all | solution.py:198
